TPU v7x, 32 devices: a whole 2x2x4 slice. The times are simulated.
32 devices in a mesh: half: 2 (over x), grp: 4 (over z), tile: 4 (over y, core).
Axes of the slice: x: 2, y: 2, z: 4, core: 2. Of those that a mesh axis runs over, the one named last changes fastest.
Arguments:
- core_tensor: bfloat16 [256, 96, 160], P(('half', 'grp', 'tile')), may hold values from -0.109375 to 0.109375
- term_operators: bfloat16 [32, 8, 8, 8], P(('half', 'grp', 'tile')), may hold values from -2 to 2
- block_terms: int32 [32, 8], P(('half', 'grp', 'tile')), may hold values from 0 to 8, as said below
- orbitals: bfloat16 [1024, 256, 256], P(('half', 'grp'), 'tile'), may hold values from -6 to 6
- potential: float32 [2, 8, 1024, 256], P(None, None, ('half', 'grp'), 'tile'), may hold values from -2.5 to 2.5
- kinetic: bfloat16 [1024, 1024], replicated, may hold values from -0.1875 to 0.1875
Outputs:
- h_orbitals: bfloat16 [1024, 256, 256], P(('half', 'grp'), 'tile')
Inputs may be any that keep to these rules, and one draw needn't show every extreme that they name: `block_terms`: each row lists distinct terms in its first slots and 8 in all later slots; every row lists at least one term, and some row lists 8 terms.
All inputs are finite; a program needn't handle non-finite values.
Results may differ from a plain program's by a relative error of at most 0.0056.
Values may be sent and summed in bfloat16 or wider, within the bound.
No kernel may reach another device: no remote copies, remote signals or barrier semaphores. Data moves between devices by JAX's collectives and lax.ppermute only.
A program may use at most 128 MiB of HBM per device.

v0:
```python
import jax
import jax.numpy as jnp
from jax import lax
from jax.sharding import PartitionSpec as P

TERMS = 8


def slot_sums(core_tensor, term_operators, block_terms):
    rows_tile, width_b, width_a = core_tensor.shape
    flat_core = core_tensor.reshape(rows_tile, width_b * width_a)
    listed = block_terms[0]
    live_slots = jnp.sum((listed < TERMS).astype(jnp.int32))
    labels = jnp.arange(TERMS, dtype=jnp.int32)

    def add_slot(slot_index, running):
        sum_a, sum_b = running
        operator = term_operators[0, slot_index]
        mixed_core = jnp.einsum(
            "rs,rq->sq", operator, flat_core, preferred_element_type=jnp.float32
        )
        mixed_core = mixed_core.astype(jnp.bfloat16).reshape(rows_tile, width_b, width_a)
        gram_a = jnp.einsum(
            "rba,rbc->ac", core_tensor, mixed_core, preferred_element_type=jnp.float32
        )
        gram_b = jnp.einsum(
            "rba,rda->bd", core_tensor, mixed_core, preferred_element_type=jnp.float32
        )
        chosen = (labels == listed[slot_index]).astype(jnp.float32)
        return (sum_a + chosen[:, None, None] * gram_a, sum_b + chosen[:, None, None] * gram_b)

    start_sums = (
        jnp.zeros((TERMS, width_a, width_a), jnp.float32),
        jnp.zeros((TERMS, width_b, width_b), jnp.float32),
    )
    return lax.fori_loop(0, live_slots, add_slot, start_sums)


def point_action(points, weights, stack_a, stack_b):
    width_a = stack_a.shape[0]
    width_b = stack_b.shape[0]
    count_points = points.shape[0]
    prod_a = jnp.dot(points[:, :width_a], stack_a, preferred_element_type=jnp.float32).reshape(
        count_points, TERMS, width_a
    )
    prod_b = jnp.dot(points[:, width_a:], stack_b, preferred_element_type=jnp.float32).reshape(
        count_points, TERMS, width_b
    )
    act_a = jnp.sum(prod_a * weights[0].T[:, :, None], axis=1)
    act_b = jnp.sum(prod_b * weights[1].T[:, :, None], axis=1)
    return jnp.concatenate([act_a, act_b], axis=1)


def kinetic_columns(kinetic, orbitals):
    rows_x, rows_y, width_all = orbitals.shape
    halves = lax.axis_size("half")
    members = lax.axis_size("grp")
    groups = halves * members
    columns = rows_y * width_all // groups
    pieces = orbitals.reshape(rows_x, groups, columns)
    applied = jnp.einsum(
        "xz,zik->xik",
        kinetic,
        lax.all_to_all(pieces, ("half", "grp"), split_axis=1, concat_axis=0, tiled=True),
        preferred_element_type=jnp.float32,
    )
    applied = applied.astype(jnp.bfloat16)
    returned = lax.all_to_all(applied, ("half", "grp"), split_axis=0, concat_axis=1, tiled=True)
    return returned.reshape(rows_x, rows_y, width_all)


def body(core_tensor, term_operators, block_terms, orbitals, potential, kinetic):
    sum_a, sum_b = slot_sums(core_tensor, term_operators, block_terms)
    total_a, total_b = lax.psum((sum_a, sum_b), ("half", "grp", "tile"))
    mean_a = total_a.astype(jnp.bfloat16)
    mean_b = total_b.astype(jnp.bfloat16)
    kinetic_part = kinetic_columns(kinetic, orbitals)
    rows_x, rows_y, width_all = orbitals.shape
    width_a = mean_a.shape[1]
    width_b = mean_b.shape[1]
    stack_a = jnp.transpose(mean_a, (1, 0, 2)).reshape(width_a, TERMS * width_a)
    stack_b = jnp.transpose(mean_b, (1, 0, 2)).reshape(width_b, TERMS * width_b)
    points = orbitals.reshape(rows_x * rows_y, width_all)
    weights = potential.reshape(2, TERMS, rows_x * rows_y)
    action = point_action(points, weights, stack_a, stack_b).reshape(rows_x, rows_y, width_all)
    return (kinetic_part.astype(jnp.float32) + action).astype(jnp.bfloat16)


def solution(mesh):
    return jax.shard_map(
        body,
        mesh=mesh,
        in_specs=(
            P(("half", "grp", "tile"), None, None),
            P(("half", "grp", "tile"), None, None, None),
            P(("half", "grp", "tile"), None),
            P(("half", "grp"), "tile", None),
            P(None, None, ("half", "grp"), "tile"),
            P(),
        ),
        out_specs=P(("half", "grp"), "tile", None),
        check_vma=False,
    )
```

profile of v0, /device:TPU:0, one launch (start us, length us, event | category | flops | bytes accessed | tf_op | source)
XLA Modules:
  0.0 330.5 jit_solution(8414382545134291300)
XLA Ops:
  0.0 7.0 %copy.53 = bf16[128,64,256]{0,2,1:T(8,128)(2,1)} copy(bf16[128,64,256]{2,1,0:T(8,128)(2,1)} %param.11) | data formatting | bytes 8388608 | tf_op args[3]
  7.0 7.4 %all-to-all-start = ((bf16[128,8,2048]{0,2,1:T(8,128)(2,1)}), bf16[128,8,2048]{0,2,1:T(8,128)(2,1)}, u32[]{:S(2)}, u32[]{:S(2)}) async-start(bf16[128,8,2048]{0,2,1:T(8,128)(2,1)} %bitcast.84), calls=%async_computation | async-start | bytes 8388608 | tf_op jit(solution)/shard_map/all_to_all | solution.py:64
  14.6 1.2 reshape.54
  16.5 1.2 broadcast_in_dim.4
  17.7 17.9 %while.13 = (s32[]{:T(128)}, f32[8,160,160]{2,1,0:T(8,128)}, f32[8,96,96]{2,1,0:T(8,128)S(1)}, s32[]{:T(128)}, s32[8]{0:T(128)S(1)}, /*index=5*/bf16[1,8,8,8]{3,...) while((s32[]{:T(128)}, f32[8,160,160]{2,1,0:T(8,128)}, ...), condition=%wide.region_2.0_spmd.clone, body=%wide.region_1.0_spmd.clone.sunk | while | flops 65560596 | bytes 4753667 | solution.py:36
  18.3 1.2 convolution_convert_fusion.2
  21.0 1.0 copy.70
  23.3 2.6 multiply_add_fusion.4
  27.0 1.2 convolution_convert_fusion.2
  29.7 1.0 copy.70
  31.9 2.6 multiply_add_fusion.4
  35.6 120.4 %all-reduce.2 = (bf16[8,96,96]{2,1,0:T(8,128)(2,1)}, bf16[8,160,160]{2,1,0:T(8,128)(2,1)}) all-reduce(f32[8,96,96]{2,1,0:T(8,128)S(1)} %get-tuple-element.55, f32[8,160,160]{2,1,0:T(8,128)} %get-tuple-element.54), channel_id=1, replica_groups=mesh['half'=2,'grp'=4,'tile'=4] {'half','grp','tile'}, use_global_device_ids=true, to_apply=%region_5.0 | all-reduce | flops 278528 | bytes 1671168 | tf_op jit(solution)/shard_map/psum | solution.py:74
  156.1 1.5 copy.58
  158.2 1.8 fusion.10
  160.4 1.0 copy.60
  162.2 1.1 copy.61
  164.3 6.4 %copy.54 = bf16[8,128,1,2048]{3,1,0,2:T(8,128)(2,1)} copy(bf16[8,128,1,2048]{1,3,0,2:T(8,128)(2,1)} %bitcast.2) | data formatting | bytes 8388608 | tf_op jit(solution)/shard_map/all_to_all | solution.py:64
  170.7 8.2 %convert_bitcast_fusion = bf16[1024,1,2048]{2,0,1:T(8,128)(2,1)} fusion(bf16[1024,1024]{1,0:T(8,128)(2,1)S(1)} %copy-done, bf16[1024,2048]{1,0:T(8,128)(2,1)} %bitcast.85), kind=kOutput, calls=%fused_computation.17 | convolution fusion | flops 4297064448 | bytes 10485760 | tf_op jit(solution)/shard_map/xz,zik->xik/dot_general | solution.py:61
  179.4 6.8 %reduce = bf16[1024,2048]{1,0:T(8,128)(2,1)} reduce(bf16[1024,1,2048]{2,0,1:T(8,128)(2,1)} %convert_bitcast_fusion, bf16[]{:T(256)} %broadcast.13), dimensions={1}, to_apply=%copy.55.reduce_sub_computation | reduce | bytes 8388610 | tf_op jit(solution)/shard_map/convert_element_type | solution.py:67
  186.2 7.8 %reshape.66 = bf16[8,2,131072]{2,1,0:T(2,128)(2,1)} reshape(bf16[1024,2048]{1,0:T(8,128)(2,1)} %reduce) | data formatting | bytes 8388608
  194.0 4.9 %all-to-all-start.1 = ((bf16[8,2,131072]{2,1,0:T(2,128)(2,1)}), bf16[8,2,131072]{2,1,0:T(2,128)(2,1)}, u32[]{:S(2)}, u32[]{:S(2)}) async-start(bf16[8,2,131072]{2,1,0:T(2,128)(2,1)} %reshape.66), calls=%async_computation.1 | async-start | bytes 8388608 | tf_op jit(solution)/shard_map/all_to_all | solution.py:68
  198.9 11.9 %fusion.7 = f32[768,8192]{1,0:T(8,128)} fusion(bf16[96,768]{1,0:T(8,128)(2,1)S(1)} %copy-done.4, bf16[8192,256]{1,0:T(8,128)(2,1)} %bitcast.82), kind=kOutput, calls=%fused_computation.18 | convolution fusion | flops 1207959552 | bytes 27410432 | tf_op jit(solution)/shard_map/dot_general | solution.py:46
  210.8 11.6 %multiply_reduce_fusion.1 = f32[8192,96]{0,1:T(8,128)} fusion(f32[8192,8,96]{0,2,1:T(8,128)} %bitcast.78, f32[8192,8]{0,1:T(8,128)S(1)} %bitcast.87), kind=kLoop, calls=%fused_computation.11 | loop fusion | flops 11796480 | bytes 28573696 | tf_op jit(solution)/shard_map/reduce_sum | solution.py:50
  222.4 18.4 %fusion.5 = f32[1280,8192]{1,0:T(8,128)} fusion(bf16[160,1280]{1,0:T(8,128)(2,1)S(1)} %reshape.55, bf16[8192,256]{1,0:T(8,128)(2,1)} %bitcast.83), kind=kOutput, calls=%fused_computation.15 | convolution fusion | flops 3355443200 | bytes 46546944 | tf_op jit(solution)/shard_map/dot_general | solution.py:43
  240.8 18.2 %multiply_reduce_fusion = f32[8192,160]{0,1:T(8,128)} fusion(f32[8192,8,160]{0,2,1:T(8,128)} %bitcast.77, f32[8192,8]{0,1:T(8,128)S(1)} %bitcast.86), kind=kLoop, calls=%fused_computation.10 | loop fusion | flops 19660800 | bytes 47448064 | tf_op jit(solution)/shard_map/reduce_sum | solution.py:49
  259.0 7.6 %pad_maximum_fusion = f32[8192,256]{0,1:T(8,128)} fusion(f32[8192,96]{0,1:T(8,128)} %multiply_reduce_fusion.1, f32[8192,160]{0,1:T(8,128)} %multiply_reduce_fusion), kind=kLoop, calls=%fused_computation.12 | loop fusion | flops 2097152 | bytes 16777216 | tf_op jit(solution)/shard_map/concatenate | solution.py:51
  266.6 9.0 %copy.62 = f32[8192,256]{1,0:T(8,128)} copy(f32[8192,256]{0,1:T(8,128)} %pad_maximum_fusion) | data formatting | bytes 16777216 | tf_op jit(solution)/shard_map/concatenate | solution.py:51
  275.6 15.8 %all-to-all-done.1 = bf16[8,2,131072]{2,1,0:T(2,128)(2,1)} async-done(((bf16[8,2,131072]{2,1,0:T(2,128)(2,1)}), bf16[8,2,131072]{2,1,0:T(2,128)(2,1)}, u32[]{:S(2)}, u32[]{:S(2)}) %all-to-all-start.1) | async-done | bytes 4194336 | tf_op jit(solution)/shard_map/all_to_all | solution.py:68
  291.4 8.9 %reshape.67 = bf16[1024,1,2048]{2,1,0:T(2,128)(2,1)} reshape(bf16[8,2,131072]{2,1,0:T(2,128)(2,1)} %all-to-all-done.1) | data formatting | bytes 8388608
  300.2 11.5 %copy.66 = f32[8,128,1,2048]{3,0,1,2:T(8,128)} copy(bf16[8,128,1,2048]{3,2,1,0:T(2,128)(2,1)} %bitcast.80) | data formatting | bytes 12582912 | tf_op jit(solution)/shard_map/convert_element_type | solution.py:86
  311.7 9.3 %reshape.61 = f32[128,64,256]{2,1,0:T(8,128)} reshape(f32[128,8,1,2048]{3,1,0,2:T(8,128)} %bitcast.81) | data formatting | bytes 16777216 | tf_op jit(solution)/shard_map/convert_element_type | solution.py:86
  321.0 9.5 %add_convert_fusion = bf16[128,64,256]{2,1,0:T(8,128)(2,1)} fusion(f32[128,64,256]{2,1,0:T(8,128)} %reshape.61, f32[128,64,256]{2,1,0:T(8,128)} %bitcast.79), kind=kLoop, calls=%fused_computation.14 | loop fusion | flops 4194304 | bytes 20971520 | tf_op jit(solution)/shard_map/convert_element_type | solution.py:86
  (36 shorter events, 10.6 us)
Async XLA Ops:
  0.0 170.7 %copy-start = (bf16[1024,1024]{1,0:T(8,128)(2,1)S(1)}, bf16[1024,1024]{1,0:T(8,128)(2,1)}, u32[]{:S(2)}) copy-start(bf16[1024,1024]{1,0:T(8,128)(2,1)} %param.13) | copy-start | bytes 6291460
  7.0 7.4 %copy-start.2 = (bf16[8,96,160]{1,2,0:T(8,128)(2,1)S(1)}, bf16[8,96,160]{1,2,0:T(8,128)(2,1)}, u32[]{:S(2)}) copy-start(bf16[8,96,160]{1,2,0:T(8,128)(2,1)} %param.8) | copy-start | bytes 737284
  7.0 8.9 %copy-start.5 = (s32[1,8]{1,0:T(1,128)S(1)}, s32[1,8]{1,0:T(1,128)}, u32[]{:S(2)}) copy-start(s32[1,8]{1,0:T(1,128)} %param.10) | copy-start | bytes 100
  7.0 157.3 %all-to-all-start = ((bf16[128,8,2048]{0,2,1:T(8,128)(2,1)}), bf16[128,8,2048]{0,2,1:T(8,128)(2,1)}, u32[]{:S(2)}, u32[]{:S(2)}) async-start(bf16[128,8,2048]{0,2,1:T(8,128)(2,1)} %bitcast.84), calls=%async_computation | async-start | bytes 8388608 | tf_op jit(solution)/shard_map/all_to_all | solution.py:64
  194.0 4.9 %copy-start.4 = (bf16[96,768]{1,0:T(8,128)(2,1)S(1)}, bf16[96,768]{1,0:T(8,128)(2,1)}, u32[]{:S(2)}) copy-start(bf16[96,768]{1,0:T(8,128)(2,1)} %reshape.58) | copy-start | bytes 442372
  194.0 97.4 %all-to-all-start.1 = ((bf16[8,2,131072]{2,1,0:T(2,128)(2,1)}), bf16[8,2,131072]{2,1,0:T(2,128)(2,1)}, u32[]{:S(2)}, u32[]{:S(2)}) async-start(bf16[8,2,131072]{2,1,0:T(2,128)(2,1)} %reshape.66), calls=%async_computation.1 | async-start | bytes 8388608 | tf_op jit(solution)/shard_map/all_to_all | solution.py:68
  198.9 11.9 %copy-start.3 = (f32[8,8192]{1,0:T(8,128)S(1)}, f32[8,8192]{1,0:T(8,128)}, u32[]{:S(2)}) copy-start(f32[8,8192]{1,0:T(8,128)} %squeeze.17) | copy-start | bytes 786436
  321.0 9.5 %copy-start.1 = (bf16[1024,1024]{1,0:T(8,128)(2,1)S(1)}, bf16[1024,1024]{1,0:T(8,128)(2,1)}, u32[]{:S(2)}) copy-start(bf16[1024,1024]{1,0:T(8,128)(2,1)} %param.13) | copy-start | bytes 6291460
where the time goes:
time: 333 us; the launch traced here: 330 us
  blocking collectives  120 us (36%)
  local copies, waits for them, and re-layouts  75.6 us (23%)
  other arithmetic  61 us (18%)
  matrix products  43.4 us (13%)
  waiting for transfers between devices  15.8 us (5%)
  starting transfers between devices  12.3 us (4%)
    psum x1, blocking collectives, body(): total_a, total_b = lax.psum((sum_a, sum_b), ('half', 'grp', 'tile'))  120 us
    unnamed x16, local copies, waits for them, and re-layouts  23.9 us
    convert_element_type x2, local copies, waits for them, and re-layouts, body(): return (kinetic_part.astype(jnp.float32) + action).astype(jnp.bfloat16)  20.7 us
    dot_general x1, matrix products, point_action(): jnp.dot(points[:, :width_a], stack_a, preferred_element_type=jnp.float32)  18.4 us
    reduce_sum x1, other arithmetic, point_action(): act_a = jnp.sum(prod_a * weights[0].T[:, :, None], axis=1)  18.2 us
    all_to_all x1, waiting for transfers between devices, kinetic_columns(): lax.all_to_all(applied, ('half', 'grp'), split_axis=0, concat_axis=1, til...  15.8 us
    dot_general x1, matrix products, point_action(): jnp.dot(points[:, width_a:], stack_b, preferred_element_type=jnp.float32)  11.9 us
    reduce_sum x1, other arithmetic, point_action(): act_b = jnp.sum(prod_b * weights[1].T[:, :, None], axis=1)  11.6 us
  transfers between devices with their start and end apart: 2, of which 1 were waited for; matrix products, arithmetic and copies ran while one was open for 32% of the time, Pallas kernels for 0%

commit v1 on v0

--- a/solution.py
+++ b/solution.py
@@ -65,7 +65,10 @@
         preferred_element_type=jnp.float32,
     )
     applied = applied.astype(jnp.bfloat16)
-    returned = lax.all_to_all(applied, ("half", "grp"), split_axis=0, concat_axis=1, tiled=True)
+    count = lax.axis_size(("half", "grp"))
+    blocks = jnp.stack(jnp.split(applied, count, axis=0), axis=0)
+    blocks = lax.all_to_all(blocks, ("half", "grp"), split_axis=0, concat_axis=0)
+    returned = jnp.concatenate(blocks, axis=1)
     return returned.reshape(rows_x, rows_y, width_all)
 
 

time: 333 us -> 316 us (0.949)
  waiting for transfers between devices: 15.8 us -> 6.64 us
  local copies, waits for them, and re-layouts: 75.6 us -> 69.3 us
    unnamed x16 -> x21, local copies, waits for them, and re-layouts: 23.9 us -> 13 us
    reshape x0 -> x1, local copies, waits for them, and re-layouts: none -> 9.24 us  [body(): point_action(points, weights, stack_a, stack_b)]
    all_to_all x1, waiting for transfers between devices: 15.8 us -> 6.64 us  [kinetic_columns(): lax.all_to_all(blocks, ('half', 'grp'), split_axis=0, concat_axis=0)]
    convert_element_type x1 -> x0, other arithmetic: 6.79 us -> none  [kinetic_columns(): applied = applied.astype(jnp.bfloat16)]
    convert_element_type x1 -> x2, other arithmetic: 9.5 us -> 16.1 us  [body(): return (kinetic_part.astype(jnp.float32) + action).astype(jnp.bfloat16)]
    convert_element_type x2, local copies, waits for them, and re-layouts: 20.7 us -> 15.8 us  [body(): return (kinetic_part.astype(jnp.float32) + action).astype(jnp.bfloat16)]
  transfers between devices with their start and end apart: 2 -> 2, of which waited for: 1 -> 1; matrix products, arithmetic and copies ran while one was open for 32% -> 36% of each run, Pallas kernels for 0% -> 0%
where the time goes in v1:
time: 316 us; the launch traced here: 314 us
  blocking collectives  120 us (38%)
  local copies, waits for them, and re-layouts  69.3 us (22%)
  other arithmetic  60.8 us (19%)
  matrix products  42.2 us (13%)
  starting transfers between devices  12.3 us (4%)
  waiting for transfers between devices  6.64 us (2%)
    psum x1, blocking collectives, body(): total_a, total_b = lax.psum((sum_a, sum_b), ('half', 'grp', 'tile'))  120 us
    dot_general x1, matrix products, point_action(): jnp.dot(points[:, :width_a], stack_a, preferred_element_type=jnp.float32)  18.4 us
    reduce_sum x1, other arithmetic, point_action(): act_a = jnp.sum(prod_a * weights[0].T[:, :, None], axis=1)  18.2 us
    convert_element_type x2, other arithmetic, body(): return (kinetic_part.astype(jnp.float32) + action).astype(jnp.bfloat16)  16.1 us
    convert_element_type x2, local copies, waits for them, and re-layouts, body(): return (kinetic_part.astype(jnp.float32) + action).astype(jnp.bfloat16)  15.8 us
    unnamed x21, local copies, waits for them, and re-layouts  13 us
    dot_general x1, matrix products, point_action(): jnp.dot(points[:, width_a:], stack_b, preferred_element_type=jnp.float32)  11.9 us
    reduce_sum x1, other arithmetic, point_action(): act_b = jnp.sum(prod_b * weights[1].T[:, :, None], axis=1)  11.6 us
  transfers between devices with their start and end apart: 2, of which 1 were waited for; matrix products, arithmetic and copies ran while one was open for 36% of the time, Pallas kernels for 0%

profile of v1, /device:TPU:0, one launch (start us, length us, event | category | flops | bytes accessed | tf_op | source)
XLA Modules:
  0.0 313.7 jit_solution(13755656041056892793)
XLA Ops:
  0.0 7.0 %copy.41 = bf16[128,64,256]{0,2,1:T(8,128)(2,1)} copy(bf16[128,64,256]{2,1,0:T(8,128)(2,1)} %param.11) | data formatting | bytes 8388608 | tf_op args[3]
  7.0 7.4 %all-to-all-start = ((bf16[128,8,2048]{0,2,1:T(8,128)(2,1)}), bf16[128,8,2048]{0,2,1:T(8,128)(2,1)}, u32[]{:S(2)}, u32[]{:S(2)}) async-start(bf16[128,8,2048]{0,2,1:T(8,128)(2,1)} %bitcast.107), calls=%async_computation | async-start | bytes 8388608 | tf_op jit(solution)/shard_map/all_to_all | solution.py:64
  14.6 1.2 reshape.67
  16.5 1.2 broadcast_in_dim.4
  17.7 18.0 %while.13 = (s32[]{:T(128)}, f32[8,160,160]{2,1,0:T(8,128)}, f32[8,96,96]{2,1,0:T(8,128)S(1)}, s32[]{:T(128)}, s32[8]{0:T(128)S(1)}, /*index=5*/bf16[1,8,8,8]{3,...) while((s32[]{:T(128)}, f32[8,160,160]{2,1,0:T(8,128)}, ...), condition=%wide.region_2.0_spmd.clone, body=%wide.region_1.0_spmd.clone.sunk | while | flops 65560596 | bytes 4753667 | solution.py:36
  18.4 1.2 convolution_convert_fusion.3
  20.1 1.0 convolution_bitcast_fusion.4
  21.1 1.0 copy.56
  23.3 2.6 multiply_add_fusion.4
  27.0 1.2 convolution_convert_fusion.3
  29.7 1.0 copy.56
  31.9 2.6 multiply_add_fusion.4
  35.7 120.3 %all-reduce.2 = (bf16[8,96,96]{2,1,0:T(8,128)(2,1)}, bf16[8,160,160]{2,1,0:T(8,128)(2,1)}) all-reduce(f32[8,96,96]{2,1,0:T(8,128)S(1)} %get-tuple-element.55, f32[8,160,160]{2,1,0:T(8,128)} %get-tuple-element.54), channel_id=1, replica_groups=mesh['half'=2,'grp'=4,'tile'=4] {'half','grp','tile'}, use_global_device_ids=true, to_apply=%region_5.0 | all-reduce | flops 278528 | bytes 1671168 | tf_op jit(solution)/shard_map/psum | solution.py:77
  156.0 1.5 copy.45
  158.2 1.8 fusion.18
  160.3 1.0 copy.47
  162.2 1.1 copy.48
  164.3 6.4 %copy.42 = bf16[8,128,1,2048]{3,1,0,2:T(8,128)(2,1)} copy(bf16[8,128,1,2048]{1,3,0,2:T(8,128)(2,1)} %bitcast.2) | data formatting | bytes 8388608 | tf_op jit(solution)/shard_map/all_to_all | solution.py:64
  170.7 6.9 %convolution_convert_fusion.1 = bf16[1024,2048]{1,0:T(8,128)(2,1)S(1)} fusion(bf16[1024,1024]{1,0:T(8,128)(2,1)S(1)} %copy-done, bf16[1024,2048]{1,0:T(8,128)(2,1)} %bitcast.108), kind=kOutput, calls=%fused_computation.17 | convolution fusion | flops 4297064448 | bytes 10485760 | tf_op jit(solution)/shard_map/xz,zik->xik/dot_general | solution.py:61
  184.2 4.9 %all-to-all-start.1 = ((bf16[8,128,1,2048]{3,1,2,0:T(8,128)(2,1)}), bf16[8,128,1,2048]{3,1,2,0:T(8,128)(2,1)}, u32[]{:S(2)}, u32[]{:S(2)}) async-start(bf16[8,128,1,2048]{3,1,2,0:T(8,128)(2,1)} %fusion.9), calls=%async_computation.1 | async-start | bytes 8388608 | tf_op jit(solution)/shard_map/all_to_all | solution.py:70
  189.1 11.9 %fusion.7 = f32[768,8192]{1,0:T(8,128)} fusion(bf16[96,768]{1,0:T(8,128)(2,1)S(1)} %copy-done.4, bf16[8192,256]{1,0:T(8,128)(2,1)} %bitcast.105), kind=kOutput, calls=%fused_computation.18 | convolution fusion | flops 1207959552 | bytes 27410432 | tf_op jit(solution)/shard_map/dot_general | solution.py:46
  201.0 11.6 %multiply_reduce_fusion.1 = f32[8192,96]{0,1:T(8,128)} fusion(f32[8192,8,96]{0,2,1:T(8,128)} %bitcast.102, f32[8192,8]{0,1:T(8,128)S(1)} %bitcast.110), kind=kLoop, calls=%fused_computation.11 | loop fusion | flops 11796480 | bytes 28573696 | tf_op jit(solution)/shard_map/reduce_sum | solution.py:50
  212.6 18.4 %fusion.5 = f32[1280,8192]{1,0:T(8,128)} fusion(bf16[160,1280]{1,0:T(8,128)(2,1)S(1)} %reshape.68, bf16[8192,256]{1,0:T(8,128)(2,1)} %bitcast.106), kind=kOutput, calls=%fused_computation.15 | convolution fusion | flops 3355443200 | bytes 46546944 | tf_op jit(solution)/shard_map/dot_general | solution.py:43
  231.1 18.2 %multiply_reduce_fusion = f32[8192,160]{0,1:T(8,128)} fusion(f32[8192,8,160]{0,2,1:T(8,128)} %bitcast.101, f32[8192,8]{0,1:T(8,128)S(1)} %bitcast.109), kind=kLoop, calls=%fused_computation.10 | loop fusion | flops 19660800 | bytes 47448064 | tf_op jit(solution)/shard_map/reduce_sum | solution.py:49
  249.3 7.6 %pad_maximum_fusion = f32[8192,256]{0,1:T(8,128)} fusion(f32[8192,96]{0,1:T(8,128)} %multiply_reduce_fusion.1, f32[8192,160]{0,1:T(8,128)} %multiply_reduce_fusion), kind=kLoop, calls=%fused_computation.12 | loop fusion | flops 2097152 | bytes 16777216 | tf_op jit(solution)/shard_map/concatenate | solution.py:51
  256.8 9.0 %copy.49 = f32[8192,256]{1,0:T(8,128)} copy(f32[8192,256]{0,1:T(8,128)} %pad_maximum_fusion) | data formatting | bytes 16777216 | tf_op jit(solution)/shard_map/concatenate | solution.py:51
  265.8 9.2 %copy.50 = f32[128,64,256]{0,2,1:T(8,128)} copy(f32[128,64,256]{2,1,0:T(8,128)} %bitcast.104) | data formatting | bytes 16777216 | tf_op jit(solution)/shard_map/reshape | solution.py:88
  275.1 6.6 %all-to-all-done.1 = bf16[8,128,1,2048]{3,1,2,0:T(8,128)(2,1)} async-done(((bf16[8,128,1,2048]{3,1,2,0:T(8,128)(2,1)}), bf16[8,128,1,2048]{3,1,2,0:T(8,128)(2,1)}, u32[]{:S(2)}, u32[]{:S(2)}) %all-to-all-start.1) | async-done | bytes 4194336 | tf_op jit(solution)/shard_map/all_to_all | solution.py:70
  281.7 6.5 %convert_bitcast_fusion = f32[128,8,1,2048]{3,0,2,1:T(8,128)} fusion(bf16[8,128,1,2048]{3,1,2,0:T(8,128)(2,1)} %all-to-all-done.1), kind=kLoop, calls=%fused_computation.13 | loop fusion | flops 2097152 | bytes 12582912 | tf_op jit(solution)/shard_map/convert_element_type | solution.py:89
  288.2 9.1 %copy.43 = f32[128,8,1,2048]{0,3,1,2:T(8,128)} copy(f32[128,8,1,2048]{3,0,2,1:T(8,128)} %convert_bitcast_fusion) | data formatting | bytes 16777216 | tf_op jit(solution)/shard_map/convert_element_type | solution.py:89
  297.3 9.6 %add_convert_fusion = bf16[128,64,256]{0,2,1:T(8,128)(2,1)} fusion(f32[128,64,256]{0,2,1:T(8,128)} %bitcast.103, f32[128,64,256]{0,2,1:T(8,128)} %copy.50), kind=kLoop, calls=%fused_computation.14 | loop fusion | flops 4194304 | bytes 20971520 | tf_op jit(solution)/shard_map/convert_element_type | solution.py:89
  307.0 6.7 %copy.51 = bf16[128,64,256]{2,1,0:T(8,128)(2,1)} copy(bf16[128,64,256]{0,2,1:T(8,128)(2,1)} %add_convert_fusion) | data formatting | bytes 8388608 | tf_op jit(solution)/shard_map/convert_element_type | solution.py:89
  (42 shorter events, 15.6 us)
Async XLA Ops:
  0.0 170.7 %copy-start = (bf16[1024,1024]{1,0:T(8,128)(2,1)S(1)}, bf16[1024,1024]{1,0:T(8,128)(2,1)}, u32[]{:S(2)}) copy-start(bf16[1024,1024]{1,0:T(8,128)(2,1)} %param.13) | copy-start | bytes 6291460
  7.0 7.4 %copy-start.2 = (bf16[8,96,160]{1,2,0:T(8,128)(2,1)S(1)}, bf16[8,96,160]{1,2,0:T(8,128)(2,1)}, u32[]{:S(2)}) copy-start(bf16[8,96,160]{1,2,0:T(8,128)(2,1)} %param.8) | copy-start | bytes 737284
  7.0 8.9 %copy-start.5 = (s32[1,8]{1,0:T(1,128)S(1)}, s32[1,8]{1,0:T(1,128)}, u32[]{:S(2)}) copy-start(s32[1,8]{1,0:T(1,128)} %param.10) | copy-start | bytes 100
  7.0 157.3 %all-to-all-start = ((bf16[128,8,2048]{0,2,1:T(8,128)(2,1)}), bf16[128,8,2048]{0,2,1:T(8,128)(2,1)}, u32[]{:S(2)}, u32[]{:S(2)}) async-start(bf16[128,8,2048]{0,2,1:T(8,128)(2,1)} %bitcast.107), calls=%async_computation | async-start | bytes 8388608 | tf_op jit(solution)/shard_map/all_to_all | solution.py:64
  184.2 4.9 %copy-start.4 = (bf16[96,768]{1,0:T(8,128)(2,1)S(1)}, bf16[96,768]{1,0:T(8,128)(2,1)}, u32[]{:S(2)}) copy-start(bf16[96,768]{1,0:T(8,128)(2,1)} %reshape.71) | copy-start | bytes 442372
  184.2 97.5 %all-to-all-start.1 = ((bf16[8,128,1,2048]{3,1,2,0:T(8,128)(2,1)}), bf16[8,128,1,2048]{3,1,2,0:T(8,128)(2,1)}, u32[]{:S(2)}, u32[]{:S(2)}) async-start(bf16[8,128,1,2048]{3,1,2,0:T(8,128)(2,1)} %fusion.9), calls=%async_computation.1 | async-start | bytes 8388608 | tf_op jit(solution)/shard_map/all_to_all | solution.py:70
  189.1 11.9 %copy-start.3 = (f32[8,8192]{1,0:T(8,128)S(1)}, f32[8,8192]{1,0:T(8,128)}, u32[]{:S(2)}) copy-start(f32[8,8192]{1,0:T(8,128)} %squeeze.17) | copy-start | bytes 786436
  297.3 16.3 %copy-start.1 = (bf16[1024,1024]{1,0:T(8,128)(2,1)S(1)}, bf16[1024,1024]{1,0:T(8,128)(2,1)}, u32[]{:S(2)}) copy-start(bf16[1024,1024]{1,0:T(8,128)(2,1)} %param.13) | copy-start | bytes 6291460
